TPU v7x, 128 devices: a whole 4x4x4 slice. The times are simulated.
128 devices in a mesh: dp: 8 (over z, core), tensor: 16 (over x, y).
Axes of the slice: x: 4, y: 4, z: 4, core: 2. Of those that a mesh axis runs over, the one named last changes fastest.
Arguments:
- residual_in: bfloat16 [1024, 4096], P('dp'), may hold values from -3 to 3
- query: bfloat16 [1024, 8192], P('dp', 'tensor'), may hold values from -130 to 130
- fresh_key: bfloat16 [1024, 4, 128], P('dp'), may hold values from -5 to 5
- fresh_value: bfloat16 [1024, 4, 128], P('dp'), may hold values from -10 to 10
- key_cache: bfloat16 [1024, 16, 128, 128], P('dp', 'tensor'), may hold values from -5 to 5, as said below
- value_cache: bfloat16 [1024, 16, 128, 128], P('dp', 'tensor'), may hold values from -10 to 10, as said below
- lengths: int32 [1024], P('dp'), may hold values from 2 to 128
- out_weight: bfloat16 [8192, 4096], P('tensor'), may hold values from -0.0625 to 0.0625
- norm_gain: float32 [4096], replicated, may hold values from 0.1 to 1.9
- expert_ids: int32 [1024, 8], P('dp'), may hold values from 0 to 127, all different within a row; in each aligned block of 128 rows (0 to 127, 128 to 255, ...) at most 16 rows name the same one
- gate_scores: float32 [1024, 8], P('dp'), may hold values from 0.05 to 1
- w_gate: bfloat16 [128, 4096, 768], P(('dp', 'tensor')), may hold values from -0.09375 to 0.09375
- w_up: bfloat16 [128, 4096, 768], P(('dp', 'tensor')), may hold values from -0.09375 to 0.09375
- w_down: bfloat16 [128, 768, 4096], P(('dp', 'tensor')), may hold values from -0.21875 to 0.21875
Outputs:
- layer_out: bfloat16 [1024, 4096], P(('dp', 'tensor'))
Inputs may be any that keep to these rules, and one draw needn't show every extreme that they name: `expert_ids`: each row names 8 different experts; among the 128 rows of one data replica (aligned blocks) no expert is named by more than 16 rows, a bound that some block reaches. `key_cache`: the copies of one key head are equal. `value_cache`: the copies of one value head are equal.
All inputs are finite; a program needn't handle non-finite values.
Results may differ from a plain program's by a relative error of at most 0.023.
Values may be sent and summed in bfloat16 or wider, within the bound.
No kernel may reach another device: no remote copies, remote signals or barrier semaphores. Data moves between devices by JAX's collectives and lax.ppermute only.
A program may use at most 128 MiB of HBM per device.

v0:
```python
import jax
import jax.numpy as jnp
from jax import lax
from jax.sharding import PartitionSpec as P


def rms_normalize(hidden, norm_gain):
    widened = hidden.astype(jnp.float32)
    spread = jnp.mean(widened * widened, axis=-1, keepdims=True)
    return (widened * lax.rsqrt(spread + 1e-06) * norm_gain).astype(jnp.bfloat16)


def shards(
    residual_in,
    query,
    fresh_key,
    fresh_value,
    key_cache,
    value_cache,
    lengths,
    out_weight,
    norm_gain,
    expert_ids,
    gate_scores,
    w_gate,
    w_up,
    w_down,
):
    row_count = residual_in.shape[0]
    head_size = key_cache.shape[3]
    tensor_width = lax.axis_size("tensor")
    column = lax.axis_index("tensor")
    kv_head = column // (tensor_width // fresh_key.shape[1])
    head_count = query.shape[1] // head_size
    score_scale = head_size ** (-0.5)
    query_rows = query.reshape(row_count, head_count, head_size)
    cached_keys = key_cache[:, 0]
    cached_values = value_cache[:, 0]
    own_key = lax.dynamic_index_in_dim(fresh_key, kv_head, 1, keepdims=False)
    own_value = lax.dynamic_index_in_dim(fresh_value, kv_head, 1, keepdims=False)
    scores = (
        jnp.einsum("rhd,rpd->rhp", query_rows, cached_keys, preferred_element_type=jnp.float32)
        * score_scale
    )
    own_score = (
        jnp.einsum("rhd,rd->rh", query_rows, own_key, preferred_element_type=jnp.float32)
        * score_scale
    )
    in_cache = (
        lax.broadcasted_iota(jnp.int32, (row_count, cached_keys.shape[1]), 1) < lengths[:, None]
    )
    scores = jnp.where(in_cache[:, None, :], scores, -1e30)
    row_max = jnp.maximum(jnp.max(scores, axis=-1), own_score)
    cache_terms = jnp.exp(scores - row_max[..., None])
    own_term = jnp.exp(own_score - row_max)
    denom = jnp.sum(cache_terms, axis=-1) + own_term
    probs = (cache_terms / denom[..., None]).astype(jnp.bfloat16)
    own_prob = (own_term / denom).astype(jnp.bfloat16)
    attended = jnp.einsum("rhp,rpd->rhd", probs, cached_values, preferred_element_type=jnp.float32)
    attended = (
        attended
        + own_prob.astype(jnp.float32)[..., None] * own_value.astype(jnp.float32)[:, None, :]
    )
    heads_out = attended.astype(jnp.bfloat16).reshape(row_count, head_count * head_size)
    share_rows = row_count // tensor_width
    first_own = column * share_rows
    proj = lax.psum(
        jnp.dot(heads_out, out_weight, preferred_element_type=jnp.float32).astype(jnp.bfloat16),
        "tensor",
    ).astype(jnp.float32)
    hidden_all = (residual_in.astype(jnp.float32) + proj).astype(jnp.bfloat16)
    normed = rms_normalize(hidden_all, norm_gain)
    hidden_own = lax.dynamic_slice_in_dim(hidden_all, first_own, share_rows, 0)
    replica_count = lax.axis_size("dp")
    experts_all = replica_count * tensor_width
    topk_count = expert_ids.shape[1]
    cap_slots = 2 * max(1, row_count * topk_count // experts_all)
    targets = lax.broadcasted_iota(jnp.int32, (replica_count,), 0) * tensor_width + column
    matches = expert_ids[:, :, None] == targets[None, None, :]
    weights = gate_scores / jnp.sum(gate_scores, axis=1, keepdims=True)
    routed = jnp.any(matches, axis=1)
    picked_weight = jnp.sum(jnp.where(matches, weights[:, :, None], 0.0), axis=1)
    slot_index = jnp.cumsum(routed.astype(jnp.int32), axis=0) - 1
    slot_ids = lax.broadcasted_iota(jnp.int32, (1, cap_slots, 1), 1)
    selector = ((slot_index.T[:, None, :] == slot_ids) & routed.T[:, None, :]).astype(jnp.bfloat16)
    outgoing = jnp.einsum(
        "bcr,rd->bcd", selector, normed, preferred_element_type=jnp.float32
    ).astype(jnp.bfloat16)
    received = lax.all_to_all(outgoing, "dp", split_axis=0, concat_axis=0, tiled=True)
    flat_rows = received.reshape(-1, received.shape[2])
    gate_part = jnp.dot(flat_rows, w_gate[0], preferred_element_type=jnp.float32)
    up_part = jnp.dot(flat_rows, w_up[0], preferred_element_type=jnp.float32)
    act = (jax.nn.silu(gate_part) * up_part).astype(jnp.bfloat16)
    result = jnp.dot(act, w_down[0], preferred_element_type=jnp.float32).astype(jnp.bfloat16)
    answered = result.reshape(received.shape)
    returned_rows = lax.all_to_all(answered, "dp", split_axis=0, concat_axis=0, tiled=True)
    gathered = jnp.einsum(
        "bcr,bcd->brd", selector, returned_rows, preferred_element_type=jnp.float32
    )
    mixture_own = lax.psum_scatter(
        jnp.sum(picked_weight.T[:, :, None] * gathered, axis=0).astype(jnp.bfloat16),
        "tensor",
        scatter_dimension=0,
        tiled=True,
    ).astype(jnp.float32)
    return (hidden_own.astype(jnp.float32) + mixture_own).astype(jnp.bfloat16)


def solution(mesh):
    placed = (
        P("dp", None),
        P("dp", "tensor"),
        P("dp", None, None),
        P("dp", None, None),
        P("dp", "tensor", None, None),
        P("dp", "tensor", None, None),
        P("dp"),
        P("tensor", None),
        P(),
        P("dp", None),
        P("dp", None),
        P(("dp", "tensor"), None, None),
        P(("dp", "tensor"), None, None),
        P(("dp", "tensor"), None, None),
    )
    return jax.shard_map(
        shards, mesh=mesh, in_specs=placed, out_specs=P(("dp", "tensor"), None), check_vma=False
    )
```

profile of v0, /device:TPU:0, one launch (start us, length us, event | category | flops | bytes accessed | tf_op | source)
XLA Modules:
  0.0 260.0 jit_solution(1109410905941494168)
XLA Ops:
  6.5 1.1 dynamic-slice_convert_fusion
  7.6 0.9 reshape.50
  8.6 0.3 fusion.54
  8.9 0.8 iota_compare_fusion.1
  9.7 4.5 %fusion.65 = (f32[128,4]{1,0:T(8,128)S(1)}, f32[128,4,128]{2,1,0:T(4,128)S(1)}) fusion(bf16[128,4,128]{2,1,0:T(4,128)(2,1)S(1)} %reshape.50, bf16[128,1,128,128]{3,2,1,0:T(8,128)(2,1)} %param.18, pred[128,128]{1,0:T(8,128)(4,1)S(1)} %iota_compare_fusion.1), kind=kOutput, calls=%fused_computation.69 | convolution fusion | flops 16973312 | bytes 4605952 | tf_op jit(solution)/shard_map/rhd,rpd->rhp/dot_general | solution.py:42
  14.3 0.1 copy.40
  14.4 0.4 fusion.45
  14.9 0.1 copy.42
  15.0 0.1 copy.43
  15.2 3.6 %fusion.31 = bf16[128,4,128]{2,1,0:T(4,128)(2,1)S(1)} fusion(bf16[128,1,128,128]{3,2,1,0:T(8,128)(2,1)} %param.19, f32[128,4,128]{2,1,0:T(4,128)S(1)} %get-tuple-element.10, f32[128,128]{1,0:T(8,128)S(1)} %bitcast.77, f32[128,4]{1,0:T(8,128)S(1)} %copy.43, f32[128,4]{1,0:T(8,128)S(1)} %copy.42, f32[128,4]{1,0:T(8,128)S(1)} %copy.40), kind=kOutput, calls=%fused_computation.25 | convolution fusion | flops 17170432 | bytes 4659200 | tf_op jit(solution)/shard_map/rhp,rpd->rhd/dot_general | solution.py:59
  18.8 1.8 convolution_convert_fusion.1
  20.8 0.2 reduce_window_sum.11
  21.0 89.0 %all-reduce.4.cloned.1.call-done = bf16[128,4096]{1,0:T(8,128)(2,1)} async-done(((bf16[128,4096]{1,0:T(8,128)(2,1)}), bf16[128,4096]{1,0:T(8,128)(2,1)}) %all-reduce.4.cloned.1.call-update) | async-done | bytes 1048592 | tf_op jit(solution)/shard_map/psum | solution.py:67
  110.1 1.7 fusion.13
  111.8 0.5 convolution_convert_fusion
  112.3 20.3 %all_to_all.10 = bf16[8,16,4096]{2,1,0:T(8,128)(2,1)S(1)} all-to-all(bf16[8,16,4096]{2,1,0:T(8,128)(2,1)S(1)} %convolution_convert_fusion), channel_id=1, replica_groups=mesh['dp'=8,'tensor'=16] {'dp'}, dimensions={0} | all-to-all | bytes 2097152 | tf_op jit(solution)/shard_map/all_to_all | solution.py:89
  132.6 3.8 %fusion.4 = f32[128,768]{1,0:T(8,128)S(1)} fusion(bf16[128,4096]{1,0:T(8,128)(2,1)S(1)} %bitcast.74, bf16[1,4096,768]{2,1,0:T(8,128)(2,1)} %param.25), kind=kOutput, calls=%fused_computation.5 | convolution fusion | flops 805306368 | bytes 7733248 | tf_op jit(solution)/shard_map/dot_general | solution.py:91
  136.4 8.1 %fusion.6 = bf16[128,4096]{1,0:T(8,128)(2,1)} fusion(bf16[1,768,4096]{2,1,0:T(8,128)(2,1)} %param.27, bf16[128,4096]{1,0:T(8,128)(2,1)S(1)} %bitcast.75, bf16[1,4096,768]{2,1,0:T(8,128)(2,1)} %param.26, f32[128,768]{1,0:T(8,128)S(1)} %fusion.4), kind=kOutput, calls=%fused_computation.7 | convolution fusion | flops 1611726848 | bytes 15073280 | tf_op jit(solution)/shard_map/dot_general | solution.py:94
  144.5 3.6 %all-to-all-start.1 = ((bf16[8,16,4096]{2,1,0:T(8,128)(2,1)}), bf16[8,16,4096]{2,1,0:T(8,128)(2,1)S(1)}, u32[]{:S(2)}, u32[]{:S(2)}) async-start(bf16[8,16,4096]{2,1,0:T(8,128)(2,1)} %bitcast.14), calls=%async_computation.1 | async-start | bytes 2097152 | tf_op jit(solution)/shard_map/all_to_all | solution.py:96
  148.2 15.7 %all-to-all-done.1 = bf16[8,16,4096]{2,1,0:T(8,128)(2,1)S(1)} async-done(((bf16[8,16,4096]{2,1,0:T(8,128)(2,1)}), bf16[8,16,4096]{2,1,0:T(8,128)(2,1)S(1)}, u32[]{:S(2)}, u32[]{:S(2)}) %all-to-all-start.1) | async-done | bytes 1048608 | tf_op jit(solution)/shard_map/all_to_all | solution.py:96
  163.9 3.5 %multiply_reduce_fusion = bf16[128,4096]{1,0:T(8,128)(2,1)} fusion(bf16[8,16,4096]{2,1,0:T(8,128)(2,1)S(1)} %all-to-all-done.1, f32[8,128]{1,0:T(8,128)S(1)} %bitcast.81, s32[8,128]{1,0:T(8,128)S(1)} %copy.45, pred[8,128]{1,0:T(8,128)(4,1)S(1)} %bitcast.80), kind=kOutput, calls=%fused_computation | convolution fusion | flops 142114816 | bytes 2106368 | tf_op jit(solution)/shard_map/bcr,bcd->brd/dot_general | solution.py:97
  167.4 0.6 dynamic-slice
  168.7 83.0 %all-reduce.6.cloned.1.call-done = bf16[128,4096]{1,0:T(8,128)(2,1)} async-done(((bf16[128,4096]{1,0:T(8,128)(2,1)}), bf16[128,4096]{1,0:T(8,128)(2,1)}) %all-reduce.6.cloned.1.call-update) | async-done | bytes 1048592
  251.6 1.5 add_convert_fusion.1
  (32 shorter events, 0.7 us)
Async XLA Ops:
  6.5 103.5 %all-reduce.4.cloned.1.call-start = ((), (), s32[]{:S(2)}) async-start(), calls=%async_computation.2 | async-start | bytes 2097152 | tf_op jit(solution)/shard_map/psum | solution.py:67
  15.2 3.6 %copy-start = (bf16[512,4096]{1,0:T(8,128)(2,1)S(1)}, bf16[512,4096]{1,0:T(8,128)(2,1)}, u32[]{:S(2)}) copy-start(bf16[512,4096]{1,0:T(8,128)(2,1)} %param.21) | copy-start | bytes 12582916
  18.8 1.8 copy-start.3
  18.8 91.3 %copy-start.1 = (bf16[128,4096]{1,0:T(8,128)(2,1)S(1)}, bf16[128,4096]{1,0:T(8,128)(2,1)}, u32[]{:S(2)}) copy-start(bf16[128,4096]{1,0:T(8,128)(2,1)} %param.14) | copy-start | bytes 3145732
  18.8 93.0 %copy-start.2 = (f32[4096]{0:T(1024)S(1)}, f32[4096]{0:T(1024)}, u32[]{:S(2)}) copy-start(f32[4096]{0:T(1024)} %param.22) | copy-start | bytes 49156
  136.4 11.7 %copy-start.4 = (f32[128,8]{0,1:T(8,128)S(1)}, f32[128,8]{0,1:T(8,128)}, u32[]{:S(2)}) copy-start(f32[128,8]{0,1:T(8,128)} %param.24) | copy-start | bytes 12292
  144.5 19.4 %all-to-all-start.1 = ((bf16[8,16,4096]{2,1,0:T(8,128)(2,1)}), bf16[8,16,4096]{2,1,0:T(8,128)(2,1)S(1)}, u32[]{:S(2)}, u32[]{:S(2)}) async-start(bf16[8,16,4096]{2,1,0:T(8,128)(2,1)} %bitcast.14), calls=%async_computation.1 | async-start | bytes 2097152 | tf_op jit(solution)/shard_map/all_to_all | solution.py:96
  148.0 103.6 %all-reduce.6.cloned.1.call-start = ((), (), s32[]{:S(2)}) async-start(), calls=%async_computation.3 | async-start | bytes 2097152
  163.9 3.5 %copy-start.5 = (u32[128]{0:T(128)S(1)}, u32[128]{0:T(128)}, u32[]{:S(2)}) copy-start(u32[128]{0:T(128)} %constant.65) | copy-start | bytes 1540
Sparse Core Ops, SparseCore 0:
  20.7 89.3 all-reduce.3
  167.6 84.0 all-reduce.5
where the time goes:
time: 260 us
  waiting for transfers between devices  188 us (72%)
  matrix products  26 us (10%)
  blocking collectives  20.3 us (8%)
  between operations  14.2 us (5%)
  other arithmetic  5.8 us (2%)
  starting transfers between devices  3.6 us (1%)
    psum x1, waiting for transfers between devices, shards(): lax.psum(jnp.dot(heads_out, out_weight, preferred_element_type=jnp.float3...  89 us
    unnamed x3, waiting for transfers between devices  83 us
    all_to_all x1, blocking collectives, shards(): lax.all_to_all(outgoing, 'dp', split_axis=0, concat_axis=0, tiled=True)  20.3 us
    all_to_all x1, waiting for transfers between devices, shards(): lax.all_to_all(answered, 'dp', split_axis=0, concat_axis=0, tiled=True)  15.7 us
    dot_general x1, matrix products, shards(): jnp.dot(act, w_down[0], preferred_element_type=jnp.float32)  8.05 us
  transfers between devices with their start and end apart: 3, of which 3 were waited for; matrix products, arithmetic and copies ran while one was open for 0% of the time, Pallas kernels for 0%

commit v1 on v0

--- a/solution.py
+++ b/solution.py
@@ -1,7 +1,15 @@
+import functools
 import jax
 import jax.numpy as jnp
 from jax import lax
 from jax.sharding import PartitionSpec as P
+
+
+def deliver_view(body, net_axis):
+    return jnp.sum(jax.lax.all_gather(body, axis_name=net_axis), axis=0)
+
+
+balance_turns = functools.partial(deliver_view, net_axis="tensor")
 
 
 def rms_normalize(hidden, norm_gain):
@@ -64,9 +72,8 @@
     heads_out = attended.astype(jnp.bfloat16).reshape(row_count, head_count * head_size)
     share_rows = row_count // tensor_width
     first_own = column * share_rows
-    proj = lax.psum(
-        jnp.dot(heads_out, out_weight, preferred_element_type=jnp.float32).astype(jnp.bfloat16),
-        "tensor",
+    proj = balance_turns(
+        jnp.dot(heads_out, out_weight, preferred_element_type=jnp.float32).astype(jnp.bfloat16)
     ).astype(jnp.float32)
     hidden_all = (residual_in.astype(jnp.float32) + proj).astype(jnp.bfloat16)
     normed = rms_normalize(hidden_all, norm_gain)

time: 260 us -> 293 us (1.13)
  waiting for transfers between devices: 188 us -> 213 us
  other arithmetic: 5.8 us -> 13.6 us
    all_gather x0 -> x1, waiting for transfers between devices: none -> 113 us  [deliver_view(): return jnp.sum(jax.lax.all_gather(body, axis_name=net_axis), axis=0)]
    psum x1 -> x0, waiting for transfers between devices: 89 us -> none  [shards(): lax.psum(jnp.dot(heads_out, out_weight, preferred_element_type=jnp.float3...]
    reduce_sum x0 -> x1, other arithmetic: none -> 8.99 us  [deliver_view(): return jnp.sum(jax.lax.all_gather(body, axis_name=net_axis), axis=0)]
where the time goes in v1:
time: 293 us
  waiting for transfers between devices  213 us (73%)
  matrix products  26 us (9%)
  blocking collectives  20.3 us (7%)
  between operations  14.2 us (5%)
  other arithmetic  13.6 us (5%)
  starting transfers between devices  3.6 us (1%)
    all_gather x1, waiting for transfers between devices, deliver_view(): return jnp.sum(jax.lax.all_gather(body, axis_name=net_axis), axis=0)  113 us
    unnamed x3, waiting for transfers between devices  83.5 us
    all_to_all x1, blocking collectives, shards(): lax.all_to_all(outgoing, 'dp', split_axis=0, concat_axis=0, tiled=True)  20.3 us
    all_to_all x1, waiting for transfers between devices, shards(): lax.all_to_all(answered, 'dp', split_axis=0, concat_axis=0, tiled=True)  15.7 us
    reduce_sum x1, other arithmetic, deliver_view(): return jnp.sum(jax.lax.all_gather(body, axis_name=net_axis), axis=0)  8.99 us
    dot_general x1, matrix products, shards(): jnp.dot(act, w_down[0], preferred_element_type=jnp.float32)  8.06 us
  transfers between devices with their start and end apart: 3, of which 3 were waited for; matrix products, arithmetic and copies ran while one was open for 0% of the time, Pallas kernels for 0%

profile of v1, /device:TPU:0, one launch (start us, length us, event | category | flops | bytes accessed | tf_op | source)
XLA Modules:
  0.0 292.6 jit_solution(5641972328492511167)
XLA Ops:
  6.5 1.1 dynamic-slice_convert_fusion
  7.6 0.9 reshape.50
  8.6 0.3 fusion.54
  8.9 0.8 iota_compare_fusion.1
  9.7 4.5 %fusion.65 = (f32[128,4]{1,0:T(8,128)S(1)}, f32[128,4,128]{2,1,0:T(4,128)S(1)}) fusion(bf16[128,4,128]{2,1,0:T(4,128)(2,1)S(1)} %reshape.50, bf16[128,1,128,128]{3,2,1,0:T(8,128)(2,1)} %param.18, pred[128,128]{1,0:T(8,128)(4,1)S(1)} %iota_compare_fusion.1), kind=kOutput, calls=%fused_computation.69 | convolution fusion | flops 16973312 | bytes 4605952 | tf_op jit(solution)/shard_map/rhd,rpd->rhp/dot_general | solution.py:50
  14.3 0.1 copy.40
  14.4 0.4 fusion.45
  14.9 0.1 copy.42
  15.2 3.6 %fusion.31 = bf16[128,4,128]{2,1,0:T(4,128)(2,1)S(1)} fusion(bf16[128,1,128,128]{3,2,1,0:T(8,128)(2,1)} %param.19, f32[128,4,128]{2,1,0:T(4,128)S(1)} %get-tuple-element.10, f32[128,128]{1,0:T(8,128)S(1)} %bitcast.79, f32[128,4]{1,0:T(8,128)S(1)} %copy.43, f32[128,4]{1,0:T(8,128)S(1)} %copy.42, f32[128,4]{1,0:T(8,128)S(1)} %copy.40), kind=kOutput, calls=%fused_computation.25 | convolution fusion | flops 17170432 | bytes 4659200 | tf_op jit(solution)/shard_map/rhp,rpd->rhd/dot_general | solution.py:67
  18.8 1.7 convolution_convert_fusion.1
  20.7 0.2 reduce_window_sum.11
  21.0 113.4 %all-gather.3.cloned.1.call-done = bf16[2048,4096]{1,0:T(8,128)(2,1)} async-done(((bf16[128,4096]{1,0:T(8,128)(2,1)}), bf16[2048,4096]{1,0:T(8,128)(2,1)}) %all-gather.3.cloned.1.call-update) | async-done | bytes 16777232 | tf_op jit(solution)/shard_map/all_gather | solution.py:9
  134.3 9.0 %reduce_sum.58 = bf16[128,4096]{1,0:T(8,128)(2,1)S(1)} reduce(bf16[16,128,4096]{2,1,0:T(8,128)(2,1)} %bitcast.75, bf16[]{:T(256)} %constant.52.clone.1), dimensions={0}, to_apply=%region_2.3 | reduce | flops 7864320 | bytes 17825794 | tf_op jit(solution)/shard_map/reduce_sum | solution.py:9
  143.3 0.5 fusion.13
  143.8 0.5 convolution_convert_fusion
  144.4 20.3 %all_to_all.10 = bf16[8,16,4096]{2,1,0:T(8,128)(2,1)S(1)} all-to-all(bf16[8,16,4096]{2,1,0:T(8,128)(2,1)S(1)} %convolution_convert_fusion), channel_id=1, replica_groups=mesh['dp'=8,'tensor'=16] {'dp'}, dimensions={0} | all-to-all | bytes 2097152 | tf_op jit(solution)/shard_map/all_to_all | solution.py:96
  164.7 3.8 %fusion.4 = f32[128,768]{1,0:T(8,128)S(1)} fusion(bf16[128,4096]{1,0:T(8,128)(2,1)S(1)} %bitcast.76, bf16[1,4096,768]{2,1,0:T(8,128)(2,1)} %param.25), kind=kOutput, calls=%fused_computation.5 | convolution fusion | flops 805306368 | bytes 7733248 | tf_op jit(solution)/shard_map/dot_general | solution.py:98
  168.5 8.1 %fusion.6 = bf16[128,4096]{1,0:T(8,128)(2,1)} fusion(bf16[1,768,4096]{2,1,0:T(8,128)(2,1)} %param.27, bf16[128,4096]{1,0:T(8,128)(2,1)S(1)} %bitcast.77, bf16[1,4096,768]{2,1,0:T(8,128)(2,1)} %param.26, f32[128,768]{1,0:T(8,128)S(1)} %fusion.4), kind=kOutput, calls=%fused_computation.7 | convolution fusion | flops 1611726848 | bytes 15073280 | tf_op jit(solution)/shard_map/dot_general | solution.py:101
  176.5 3.6 %all-to-all-start.1 = ((bf16[8,16,4096]{2,1,0:T(8,128)(2,1)}), bf16[8,16,4096]{2,1,0:T(8,128)(2,1)S(1)}, u32[]{:S(2)}, u32[]{:S(2)}) async-start(bf16[8,16,4096]{2,1,0:T(8,128)(2,1)} %bitcast.15), calls=%async_computation.1 | async-start | bytes 2097152 | tf_op jit(solution)/shard_map/all_to_all | solution.py:103
  180.3 15.7 %all-to-all-done.1 = bf16[8,16,4096]{2,1,0:T(8,128)(2,1)S(1)} async-done(((bf16[8,16,4096]{2,1,0:T(8,128)(2,1)}), bf16[8,16,4096]{2,1,0:T(8,128)(2,1)S(1)}, u32[]{:S(2)}, u32[]{:S(2)}) %all-to-all-start.1) | async-done | bytes 1048608 | tf_op jit(solution)/shard_map/all_to_all | solution.py:103
  196.0 3.5 %multiply_reduce_fusion = bf16[128,4096]{1,0:T(8,128)(2,1)} fusion(bf16[8,16,4096]{2,1,0:T(8,128)(2,1)S(1)} %all-to-all-done.1, f32[8,128]{1,0:T(8,128)S(1)} %bitcast.83, s32[8,128]{1,0:T(8,128)S(1)} %copy.45, pred[8,128]{1,0:T(8,128)(4,1)S(1)} %bitcast.82), kind=kOutput, calls=%fused_computation | convolution fusion | flops 142114816 | bytes 2106368 | tf_op jit(solution)/shard_map/bcr,bcd->brd/dot_general | solution.py:104
  199.5 0.6 dynamic-slice
  200.8 83.5 %all-reduce.3.cloned.1.call-done = bf16[128,4096]{1,0:T(8,128)(2,1)} async-done(((bf16[128,4096]{1,0:T(8,128)(2,1)}), bf16[128,4096]{1,0:T(8,128)(2,1)}) %all-reduce.3.cloned.1.call-update) | async-done | bytes 1048592
  284.3 1.5 add_convert_fusion.1
  (33 shorter events, 0.8 us)
Async XLA Ops:
  6.5 127.8 %all-gather.3.cloned.1.call-start = ((), (), s32[]{:S(2)}) async-start(), calls=%async_computation.2 | async-start | bytes 17825792 | tf_op jit(solution)/shard_map/all_gather | solution.py:9
  15.2 3.6 %copy-start = (bf16[512,4096]{1,0:T(8,128)(2,1)S(1)}, bf16[512,4096]{1,0:T(8,128)(2,1)}, u32[]{:S(2)}) copy-start(bf16[512,4096]{1,0:T(8,128)(2,1)} %param.21) | copy-start | bytes 12582916
  18.8 1.8 copy-start.3
  134.3 9.0 %copy-start.1 = (bf16[128,4096]{1,0:T(8,128)(2,1)S(1)}, bf16[128,4096]{1,0:T(8,128)(2,1)}, u32[]{:S(2)}) copy-start(bf16[128,4096]{1,0:T(8,128)(2,1)} %param.14) | copy-start | bytes 3145732
  134.3 9.5 %copy-start.2 = (f32[4096]{0:T(1024)S(1)}, f32[4096]{0:T(1024)}, u32[]{:S(2)}) copy-start(f32[4096]{0:T(1024)} %param.22) | copy-start | bytes 49156
  168.5 11.7 %copy-start.4 = (f32[128,8]{0,1:T(8,128)S(1)}, f32[128,8]{0,1:T(8,128)}, u32[]{:S(2)}) copy-start(f32[128,8]{0,1:T(8,128)} %param.24) | copy-start | bytes 12292
  176.5 19.4 %all-to-all-start.1 = ((bf16[8,16,4096]{2,1,0:T(8,128)(2,1)}), bf16[8,16,4096]{2,1,0:T(8,128)(2,1)S(1)}, u32[]{:S(2)}, u32[]{:S(2)}) async-start(bf16[8,16,4096]{2,1,0:T(8,128)(2,1)} %bitcast.15), calls=%async_computation.1 | async-start | bytes 2097152 | tf_op jit(solution)/shard_map/all_to_all | solution.py:103
  180.1 104.2 %all-reduce.3.cloned.1.call-start = ((), (), s32[]{:S(2)}) async-start(), calls=%async_computation.3 | async-start | bytes 2097152
  196.0 3.5 %copy-start.5 = (u32[128]{0:T(128)S(1)}, u32[128]{0:T(128)}, u32[]{:S(2)}) copy-start(u32[128]{0:T(128)} %constant.67) | copy-start | bytes 1540
Sparse Core Ops, SparseCore 0:
  20.6 113.6 all-gather.2
  199.6 84.5 all-reduce.2
